TPU v7x, 256 devices: a whole 4x4x8 slice. The times are simulated.
256 devices in a mesh: region: 8 (over x, core), dom: 32 (over z, y).
Axes of the slice: x: 4, y: 4, z: 8, core: 2. Of those that a mesh axis runs over, the one named last changes fastest.
Arguments:
- x_init: bfloat16 [1048576, 128], P(('region', 'dom')), may hold values from -6 to 6
- tiles: bfloat16 [73728, 128, 128], P(('region', 'dom'))
- tile_row: int32 [73728], P(('region', 'dom')), may hold values from 0 to 31
- tile_col: int32 [73728], P(('region', 'dom')), may hold values from 0 to 63, as said below
- send_list: int32 [256, 4, 8], P(('region', 'dom')), may hold values from 0 to 31, as said below
- send_count: int32 [256, 4], P(('region', 'dom')), may hold values from 1 to 8, as said below
Outputs:
- basis: bfloat16 [1048576, 128], P(('region', 'dom'))
- ritz_matrix: float32 [2, 128, 128], replicated
Inputs may be any that keep to these rules, and one draw needn't show every extreme that they name: `send_list`: the 8 entries of one partition and direction are distinct row tiles of that partition. `send_count`: some partition sends 8 row tiles in every direction. `tile_col`: a value 32 + d * 8 + s with d = 0 .. 3 names slot s of the d-th received stack of extended, and s is below the count that this neighbour sends; no value names a stack where the neighbour does not exist.
All inputs are finite; a program needn't handle non-finite values.
Results may differ from a plain program's by a relative error of at most 0.00115.
The roundings to bfloat16 on the way count: a program that leaves them out, or rounds other values in their place, can miss the bound.
Values may be sent and summed in bfloat16 or wider, within the bound.
No kernel may reach another device: no remote copies, remote signals or barrier semaphores. Data moves between devices by JAX's collectives and lax.ppermute only.
A program may use at most 64 MiB of HBM per device.

v0:
```python
import math
import jax
import jax.numpy as jnp
from jax import lax
from jax.sharding import PartitionSpec as P

ITERS = 2
HIGH = lax.Precision.HIGHEST


def shifted(block, axis, distance):
    devices = range(lax.axis_size(axis))
    route = [(i - distance, i) for i in devices if i - distance in devices]
    return lax.ppermute(block, axis, route)


def local_gram(current, node_total):
    return (
        lax.dot_general(
            current, current, (((0,), (0,)), ((), ())), preferred_element_type=jnp.float32
        )
        / node_total
    )


def rayleigh_sum(partial_value):
    return lax.psum(partial_value, ("region", "dom"))


def pass_dom(packed, offset):
    return shifted(packed, "dom", offset)


def pass_region(packed, offset):
    return shifted(packed, "region", offset)


def apply_graph(basis, tiles, tile_row, tile_col, send_rows, live_slot, row_tiles, tile_size):
    vectors = basis.shape[1]
    blocks = basis.reshape(row_tiles, tile_size, vectors)
    picked = blocks[send_rows]
    packed = jnp.where(live_slot[:, :, None, None], picked, jnp.zeros_like(picked))
    received = [
        pass_dom(packed[0], 1),
        pass_dom(packed[1], -1),
        pass_region(packed[2], 1),
        pass_region(packed[3], -1),
    ]
    extended = jnp.concatenate([blocks] + received, axis=0)
    group = 32
    group_count = tiles.shape[0] // group
    tile_groups = tiles.reshape(group_count, group, tile_size, tile_size)
    col_groups = tile_col.reshape(group_count, group)
    row_groups = tile_row.reshape(group_count, group)
    row_ids = jnp.arange(row_tiles, dtype=jnp.int32)

    def add_group(accumulated, pieces):
        tile_part, col_part, row_part = pieces
        gathered = extended[col_part]
        products = lax.dot_general(
            tile_part, gathered, (((2,), (1,)), ((0,), (0,))), preferred_element_type=jnp.float32
        )
        select = (row_part[None, :] == row_ids[:, None]).astype(jnp.float32)
        return (accumulated + jnp.einsum("rt,tiw->riw", select, products, precision=HIGH), None)

    start = jnp.zeros((row_tiles, tile_size, vectors), jnp.float32)
    applied, _ = lax.scan(add_group, start, (tile_groups, col_groups, row_groups))
    return applied.reshape(row_tiles * tile_size, vectors)


def shards(x_init, tiles, tile_row, tile_col, send_list, send_count):
    row_count, vectors = x_init.shape
    tile_size = tiles.shape[1]
    row_tiles = row_count // tile_size
    capacity = send_list.shape[2]
    node_total = row_count * lax.axis_size("region") * lax.axis_size("dom")
    root_total = math.sqrt(node_total)
    send_rows = send_list[0]
    live_slot = jnp.arange(capacity, dtype=jnp.int32)[None, :] < send_count[0][:, None]
    identity = jnp.eye(vectors, dtype=jnp.float32)
    current = x_init
    gram = lax.psum(local_gram(current, node_total), ("region", "dom"))
    rayleigh_list = []
    basis = x_init
    for iteration in range(ITERS):
        factor = jnp.linalg.cholesky(gram)
        inverse = lax.linalg.triangular_solve(factor, identity, left_side=True, lower=True)
        basis = jnp.dot(current.astype(jnp.float32), inverse.T, precision=HIGH).astype(jnp.bfloat16)
        applied = apply_graph(
            basis, tiles, tile_row, tile_col, send_rows, live_slot, row_tiles, tile_size
        )
        partial_value = jnp.dot(basis.astype(jnp.float32).T, applied, precision=HIGH) / root_total
        if iteration + 1 < ITERS:
            current = applied.astype(jnp.bfloat16)
            rayleigh_list.append(rayleigh_sum(partial_value))
            gram = lax.psum(local_gram(current, node_total), ("region", "dom"))
        else:
            rayleigh_list.append(rayleigh_sum(partial_value))
    return (basis, jnp.stack(rayleigh_list))


def solution(mesh):
    in_specs = (
        P(("region", "dom"), None),
        P(("region", "dom"), None, None),
        P(("region", "dom")),
        P(("region", "dom")),
        P(("region", "dom"), None, None),
        P(("region", "dom"), None),
    )
    out_specs = (P(("region", "dom"), None), P())
    return jax.shard_map(shards, mesh=mesh, in_specs=in_specs, out_specs=out_specs, check_vma=False)
```

profile of v0, /device:TPU:2, one launch (start us, length us, event | category | flops | bytes accessed | tf_op | source)
XLA Modules:
  0.0 1021.1 jit_solution(12112515196211047036)
XLA Ops:
  9.8 247.8 %all-reduce.5.cloned.1.call-done = f32[128,128]{0,1:T(8,128)} async-done(((f32[128,128]{0,1:T(8,128)}), f32[128,128]{0,1:T(8,128)}) %all-reduce.5.cloned.1.call-update) | async-done | bytes 65552 | tf_op jit(solution)/shard_map/psum | solution.py:82
  259.4 11.7 %cholesky.44 = f32[128,128]{1,0:T(8,128)S(1)} custom-call(f32[128,128]{1,0:T(8,128)S(1)} %fusion.46), custom_call_target="Cholesky" | custom-call | tf_op jit(solution)/shard_map/jit(cholesky)/cholesky | solution.py:86
  272.4 9.8 custom-call.8
  295.1 3.3 collective-permute-start.3
  298.5 3.4 collective-permute-done.1
  303.6 82.5 %while.22 = (s32[]{:T(128)}, f32[32,128,128]{2,0,1:T(8,128)}, s32[9,32]{1,0:T(8,128)S(1)}, bf16[9,32,128,128]{3,2,1,0:T(8,128)(2,1)}, s32[9,32]{1,0:T(8,128)S(1)...) while((s32[]{:T(128)}, f32[32,128,128]{2,0,1:T(8,128)}, s32[9,32]{1,0:T(8,128)S(1)}, ...), condition=%wide.region_4.7_spmd.clone, body=%wide.region_3.6_spmd.clone.sunk | while | flops 336595040 | bytes 29365292 | solution.py:67
  307.8 3.5 select_add_fusion.4
  317.0 3.5 select_add_fusion.4
  326.2 3.5 select_add_fusion.4
  335.4 3.5 select_add_fusion.4
  344.5 3.5 select_add_fusion.4
  353.7 3.5 select_add_fusion.4
  362.9 3.5 select_add_fusion.4
  372.0 3.5 select_add_fusion.4
  381.2 3.5 select_add_fusion.4
  386.1 3.5 fusion.32
  392.2 239.2 %all-reduce.7.cloned.1.call-done = f32[128,128]{0,1:T(8,128)} async-done(((f32[128,128]{0,1:T(8,128)}), f32[128,128]{0,1:T(8,128)}) %all-reduce.7.cloned.1.call-update) | async-done | bytes 65552 | tf_op jit(solution)/shard_map/psum | solution.py:96
  633.2 11.7 %cholesky.55 = f32[128,128]{1,0:T(8,128)S(1)} custom-call(f32[128,128]{1,0:T(8,128)S(1)} %fusion.44), custom_call_target="Cholesky" | custom-call | tf_op jit(solution)/shard_map/jit(cholesky)/cholesky | solution.py:86
  646.3 9.8 custom-call.9
  661.5 4.6 collective-permute-start.4
  670.0 3.9 collective-permute-start.7
  678.8 82.3 %while.23 = (s32[]{:T(128)}, f32[32,128,128]{2,0,1:T(8,128)}, s32[9,32]{1,0:T(8,128)S(1)}, bf16[9,32,128,128]{3,2,1,0:T(8,128)(2,1)}, s32[9,32]{1,0:T(8,128)S(1)...) while((s32[]{:T(128)}, f32[32,128,128]{2,0,1:T(8,128)}, s32[9,32]{1,0:T(8,128)S(1)}, ...), condition=%wide.region_8.11_spmd.clone, body=%wide.region_7.10_spmd.clone.sunk | while | flops 336595040 | bytes 29365292 | solution.py:67
  683.1 3.5 select_add_fusion.5
  692.2 3.5 select_add_fusion.5
  701.4 3.5 select_add_fusion.5
  710.5 3.5 select_add_fusion.5
  719.7 3.5 select_add_fusion.5
  728.8 3.5 select_add_fusion.5
  738.0 3.5 select_add_fusion.5
  747.1 3.5 select_add_fusion.5
  756.3 3.5 select_add_fusion.5
  766.0 247.0 %all-reduce.9.cloned.1.call-done = (f32[1,128,128]{2,1,0:T(8,128)}, f32[1,128,128]{2,1,0:T(8,128)}) async-done(((f32[1,128,128]{2,1,0:T(8,128)}, f32[1,128,128]{2,1,0:T(8,128)}), (f32[1,128,128]{2,1,0:T(8,128)}, f32[1,128,128]{2,1,0:T(8,128)})) %all-reduce.9.cloned.1.call-update) | async-done | bytes 131088 | tf_op jit(solution)/shard_map/psum | solution.py:27
  (249 shorter events, 147.0 us)
Async XLA Ops:
  7.2 2.4 copy-start.15
  7.2 2.5 copy-start.14
  7.2 250.4 %all-reduce.5.cloned.1.call-start = ((), (), s32[]{:S(2)}) async-start(), calls=%async_computation | async-start | bytes 131072 | tf_op jit(solution)/shard_map/psum | solution.py:82
  9.5 621.9 %all-reduce.7.cloned.1.call-start = ((), (), s32[]{:S(2)}) async-start(), calls=%async_computation.1 | async-start | bytes 131072 | tf_op jit(solution)/shard_map/psum | solution.py:96
  283.5 2.3 copy-start.10
  285.9 6.6 copy-start.12
  285.9 6.7 copy-start.13
  288.2 10.3 %collective-permute-start = (bf16[8,128,128]{2,1,0:T(8,128)(2,1)}, bf16[8,128,128]{2,1,0:T(8,128)(2,1)S(1)}, u32[]{:S(2)}, u32[]{:S(2)}) collective-permute-start(bf16[8,128,128]{2,1,0:T(8,128)(2,1)} %get-tuple-element.159), channel_id=1, source_target_pairs={{0,1},{1,2},{2,3},{3,4},{4,5},{5,6},{6,7},{7,8},{8,9},{9,10},{10,1... | collective-permute-start | bytes 786440 | tf_op jit(solution)/shard_map/ppermute | solution.py:14
  291.2 10.8 %collective-permute-start.1 = (bf16[8,128,128]{2,1,0:T(8,128)(2,1)}, bf16[8,128,128]{2,1,0:T(8,128)(2,1)S(1)}, u32[]{:S(2)}, u32[]{:S(2)}) collective-permute-start(bf16[8,128,128]{2,1,0:T(8,128)(2,1)} %get-tuple-element.158), channel_id=1, source_target_pairs={{1,0},{2,1},{3,2},{4,3},{5,4},{6,5},{7,6},{8,7},{9,8},{10,9},{11,1... | collective-permute-start | bytes 786440 | tf_op jit(solution)/shard_map/ppermute | solution.py:14
  292.6 9.4 collective-permute-start.2
  295.1 7.0 collective-permute-start.3
  305.9 1.9 copy-start.1
  315.1 1.9 copy-start.1
  324.3 1.9 copy-start.1
  333.4 1.9 copy-start.1
  342.6 1.9 copy-start.1
  351.8 1.9 copy-start.1
  360.9 1.9 copy-start.1
  386.1 3.6 copy-start.3
  389.6 623.4 %all-reduce.9.cloned.1.call-start = ((), (), s32[]{:S(2)}) async-start(), calls=%async_computation.2 | async-start | bytes 262144 | tf_op jit(solution)/shard_map/psum | solution.py:27
  659.0 105.0 %copy-start.9 = (bf16[4096,128]{1,0:T(8,128)(2,1)}, bf16[4096,128]{1,0:T(8,128)(2,1)S(1)}, u32[]{:S(2)}) copy-start(bf16[4096,128]{1,0:T(8,128)(2,1)S(1)} %convolution_convert_fusion) | copy-start | bytes 3145732
  659.7 6.3 copy-start.8
  659.8 6.3 copy-start.11
  660.0 13.9 %collective-permute-start.5 = (bf16[8,128,128]{2,1,0:T(8,128)(2,1)S(1)}, bf16[8,128,128]{2,1,0:T(8,128)(2,1)S(1)}, u32[]{:S(2)}, u32[]{:S(2)}) collective-permute-start(bf16[8,128,128]{2,1,0:T(8,128)(2,1)S(1)} %get-tuple-element.154), channel_id=1, source_target_pairs={{1,0},{2,1},{3,2},{4,3},{5,4},{6,5},{7,6},{8,7},{9,8},{10,9},{11,1... | collective-permute-start | bytes 786440 | tf_op jit(solution)/shard_map/ppermute | solution.py:14
  661.5 12.4 %collective-permute-start.4 = (bf16[8,128,128]{2,1,0:T(8,128)(2,1)S(1)}, bf16[8,128,128]{2,1,0:T(8,128)(2,1)S(1)}, u32[]{:S(2)}, u32[]{:S(2)}) collective-permute-start(bf16[8,128,128]{2,1,0:T(8,128)(2,1)S(1)} %get-tuple-element.155), channel_id=1, source_target_pairs={{0,1},{1,2},{2,3},{3,4},{4,5},{5,6},{6,7},{7,8},{8,9},{9,10},{10,1... | collective-permute-start | bytes 786440 | tf_op jit(solution)/shard_map/ppermute | solution.py:14
  667.9 7.7 collective-permute-start.6
  670.0 7.5 collective-permute-start.7
  681.2 1.9 copy-start.4
  690.3 1.9 copy-start.4
  726.9 1.9 copy-start.4
  736.1 1.9 copy-start.4
  745.2 1.9 copy-start.4
  (27 other events, 39.6 us)
Sparse Core Ops, SparseCore 0:
  14.1 243.4 all-reduce.4
  389.7 241.6 all-reduce.6
  766.1 246.8 all-reduce.8
where the time goes:
time: 1020 us
  waiting for transfers between devices  741 us (73%)
  matrix products  108 us (11%)
  local copies, waits for them, and re-layouts  83.8 us (8%)
  other arithmetic  50.8 us (5%)
  starting transfers between devices  21.9 us (2%)
  between operations  14.2 us (1%)
    psum x2, waiting for transfers between devices, shards(): gram = lax.psum(local_gram(current, node_total), ('region', 'dom'))  487 us
    psum x1, waiting for transfers between devices, rayleigh_sum(): return lax.psum(partial_value, ('region', 'dom'))  247 us
    dot_general x18, matrix products, add_group(): jnp.einsum('rt,tiw->riw', select, products, precision=HIGH)  63.3 us
    gather x18, local copies, waits for them, and re-layouts, add_group(): gathered = extended[col_part]  42.1 us
    dot_general x18, matrix products, add_group(): lax.dot_general(tile_part, gathered, (((2,), (1,)), ((0,), (0,))), prefer...  32.4 us
    while x72, local copies, waits for them, and re-layouts  25.8 us
    another operation x6, other arithmetic, shards(): factor = jnp.linalg.cholesky(gram)  24.8 us
    ppermute x8, starting transfers between devices, shifted(): return lax.ppermute(block, axis, route)  21.8 us
  transfers between devices with their start and end apart: 11, of which 7 were waited for; matrix products, arithmetic and copies ran while one was open for 1% of the time, Pallas kernels for 0%

commit v1 on v0

--- a/solution.py
+++ b/solution.py
@@ -93,7 +93,9 @@
         if iteration + 1 < ITERS:
             current = applied.astype(jnp.bfloat16)
             rayleigh_list.append(rayleigh_sum(partial_value))
-            gram = lax.psum(local_gram(current, node_total), ("region", "dom"))
+            gram = jnp.sum(
+                lax.all_gather(local_gram(current, node_total), ("region", "dom")), axis=0
+            )
         else:
             rayleigh_list.append(rayleigh_sum(partial_value))
     return (basis, jnp.stack(rayleigh_list))

time: 1020 us -> 940 us (0.922)
  waiting for transfers between devices: 741 us -> 633 us
  matrix products: 108 us -> 135 us
    psum x2 -> x1, waiting for transfers between devices: 487 us -> 248 us  [shards(): gram = lax.psum(local_gram(current, node_total), ('region', 'dom'))]
    all_gather x0 -> x1, waiting for transfers between devices: none -> 135 us  [shards(): lax.all_gather(local_gram(current, node_total), ('region', 'dom'))]
    dot_general x18, matrix products: 63.3 us -> 94.5 us  [add_group(): jnp.einsum('rt,tiw->riw', select, products, precision=HIGH)]
    while x72 -> x0, local copies, waits for them, and re-layouts: 25.8 us -> none
    unnamed x32 -> x33, local copies, waits for them, and re-layouts: 4.23 us -> 21.9 us
  transfers between devices with their start and end apart: 11 -> 11, of which waited for: 7 -> 5; matrix products, arithmetic and copies ran while one was open for 1% -> 1% of each run, Pallas kernels for 0% -> 0%
where the time goes in v1:
time: 940 us; the launch traced here: 937 us
  waiting for transfers between devices  633 us (67%)
  matrix products  135 us (14%)
  local copies, waits for them, and re-layouts  75.7 us (8%)
  other arithmetic  58.3 us (6%)
  starting transfers between devices  20.6 us (2%)
  between operations  14.1 us (2%)
    psum x1, waiting for transfers between devices, shards(): gram = lax.psum(local_gram(current, node_total), ('region', 'dom'))  248 us
    psum x1, waiting for transfers between devices, rayleigh_sum(): return lax.psum(partial_value, ('region', 'dom'))  247 us
    all_gather x1, waiting for transfers between devices, shards(): lax.all_gather(local_gram(current, node_total), ('region', 'dom'))  135 us
    dot_general x18, matrix products, add_group(): jnp.einsum('rt,tiw->riw', select, products, precision=HIGH)  94.5 us
    gather x18, local copies, waits for them, and re-layouts, add_group(): gathered = extended[col_part]  42.1 us
    dot_general x18, matrix products, add_group(): lax.dot_general(tile_part, gathered, (((2,), (1,)), ((0,), (0,))), prefer...  29.8 us
    another operation x6, other arithmetic, shards(): factor = jnp.linalg.cholesky(gram)  24.8 us
    unnamed x33, local copies, waits for them, and re-layouts  21.9 us
  transfers between devices with their start and end apart: 11, of which 5 were waited for; matrix products, arithmetic and copies ran while one was open for 1% of the time, Pallas kernels for 0%

profile of v1, /device:TPU:2, one launch (start us, length us, event | category | flops | bytes accessed | tf_op | source)
XLA Modules:
  0.0 937.5 jit_solution(10605159129228070745)
XLA Ops:
  9.8 247.8 %all-reduce.4.cloned.1.call-done = f32[128,128]{0,1:T(8,128)} async-done(((f32[128,128]{0,1:T(8,128)}), f32[128,128]{0,1:T(8,128)}) %all-reduce.4.cloned.1.call-update) | async-done | bytes 65552 | tf_op jit(solution)/shard_map/psum | solution.py:82
  259.4 11.7 %cholesky.44 = f32[128,128]{1,0:T(8,128)S(1)} custom-call(f32[128,128]{1,0:T(8,128)S(1)} %fusion.46), custom_call_target="Cholesky" | custom-call | tf_op jit(solution)/shard_map/jit(cholesky)/cholesky | solution.py:86
  272.4 9.8 %custom-call.8 = f32[1,128,128]{1,2,0:T(8,128)S(1)} custom-call(f32[1,128,128]{2,1,0:T(8,128)S(1)} %fusion.41), custom_call_target="InvertDiagBlocksLowerTriangular" | custom-call | tf_op jit(solution)/shard_map/triangular_solve/custom-call.0 | solution.py:87
  301.1 83.7 %while.22 = (s32[]{:T(128)}, f32[32,128,128]{2,0,1:T(8,128)}, s32[9,32]{1,0:T(8,128)S(1)}, bf16[9,32,128,128]{3,2,1,0:T(8,128)(2,1)}, s32[9,32]{1,0:T(8,128)S(1)...) while((s32[]{:T(128)}, f32[32,128,128]{2,0,1:T(8,128)}, s32[9,32]{1,0:T(8,128)S(1)}, ...), condition=%wide.region_4.7_spmd.clone, body=%wide.region_3.6_spmd.clone.sunk | while | flops 336595040 | bytes 12588519 | solution.py:67
  305.1 3.8 select_add_fusion.4
  313.0 5.4 select_add_fusion.4
  322.5 5.4 select_add_fusion.4
  332.0 5.4 select_add_fusion.4
  341.4 5.4 select_add_fusion.4
  350.9 5.4 select_add_fusion.4
  360.4 5.4 select_add_fusion.4
  369.9 5.4 select_add_fusion.4
  379.4 5.4 select_add_fusion.4
  384.8 3.5 fusion.32
  391.0 134.6 %all-gather.3.cloned.1.call-done = f32[32768,128]{0,1:T(8,128)} async-done(((f32[128,128]{0,1:T(8,128)}), f32[32768,128]{0,1:T(8,128)}) %all-gather.3.cloned.1.call-update) | async-done | bytes 16777232 | tf_op jit(solution)/shard_map/all_gather | solution.py:97
  525.6 14.1 %copy.34 = f32[16,8,256,128]{3,2,1,0:T(8,128)} copy(f32[16,8,256,128]{3,1,2,0:T(8,128)} %bitcast.131) | data formatting | bytes 33554432
  539.7 8.2 bitcast_reduce_fusion
  548.0 11.7 %cholesky.55 = f32[128,128]{1,0:T(8,128)S(1)} custom-call(f32[128,128]{1,0:T(8,128)S(1)} %fusion.44), custom_call_target="Cholesky" | custom-call | tf_op jit(solution)/shard_map/jit(cholesky)/cholesky | solution.py:86
  561.1 9.8 %custom-call.9 = f32[1,128,128]{1,2,0:T(8,128)S(1)} custom-call(f32[1,128,128]{2,1,0:T(8,128)S(1)} %fusion.42), custom_call_target="InvertDiagBlocksLowerTriangular" | custom-call | tf_op jit(solution)/shard_map/triangular_solve/custom-call.0 | solution.py:87
  575.4 3.4 collective-permute-start.4
  585.3 3.6 collective-permute-start.7
  593.5 83.6 %while.23 = (s32[]{:T(128)}, f32[32,128,128]{2,0,1:T(8,128)}, s32[9,32]{1,0:T(8,128)S(1)}, bf16[9,32,128,128]{3,2,1,0:T(8,128)(2,1)}, s32[9,32]{1,0:T(8,128)S(1)...) while((s32[]{:T(128)}, f32[32,128,128]{2,0,1:T(8,128)}, s32[9,32]{1,0:T(8,128)S(1)}, ...), condition=%wide.region_8.11_spmd.clone, body=%wide.region_7.10_spmd.clone.sunk | while | flops 336595040 | bytes 12588519 | solution.py:67
  597.6 3.8 select_add_fusion.5
  605.5 5.4 select_add_fusion.5
  614.9 5.4 select_add_fusion.5
  624.4 5.4 select_add_fusion.5
  633.9 5.4 select_add_fusion.5
  643.3 5.4 select_add_fusion.5
  652.8 5.4 select_add_fusion.5
  662.3 5.4 select_add_fusion.5
  671.7 5.4 select_add_fusion.5
  682.1 247.3 %all-reduce.6.cloned.1.call-done = (f32[1,128,128]{2,1,0:T(8,128)}, f32[1,128,128]{2,1,0:T(8,128)}) async-done(((f32[1,128,128]{2,1,0:T(8,128)}, f32[1,128,128]{2,1,0:T(8,128)}), (f32[1,128,128]{2,1,0:T(8,128)}, f32[1,128,128]{2,1,0:T(8,128)})) %all-reduce.6.cloned.1.call-update) | async-done | bytes 131088 | tf_op jit(solution)/shard_map/psum | solution.py:27
  (179 shorter events, 122.9 us)
Async XLA Ops:
  7.2 1.2 copy-start
  7.2 2.4 copy-start.10
  7.2 2.5 copy-start.11
  7.2 250.4 %all-reduce.4.cloned.1.call-start = ((), (), s32[]{:S(2)}) async-start(), calls=%async_computation | async-start | bytes 131072 | tf_op jit(solution)/shard_map/psum | solution.py:82
  9.5 516.1 %all-gather.3.cloned.1.call-start = ((), (), s32[]{:S(2)}) async-start(), calls=%async_computation.1 | async-start | bytes 16842752 | tf_op jit(solution)/shard_map/all_gather | solution.py:97
  283.5 1.4 copy-start.6
  285.0 4.6 copy-start.8
  285.0 4.6 copy-start.9
  285.2 11.3 %collective-permute-start = (bf16[8,128,128]{2,1,0:T(8,128)(2,1)S(1)}, bf16[8,128,128]{2,1,0:T(8,128)(2,1)S(1)}, u32[]{:S(2)}, u32[]{:S(2)}) collective-permute-start(bf16[8,128,128]{2,1,0:T(8,128)(2,1)S(1)} %get-tuple-element.159), channel_id=1, source_target_pairs={{0,1},{1,2},{2,3},{3,4},{4,5},{5,6},{6,7},{7,8},{8,9},{9,10},{10,1... | collective-permute-start | bytes 786440 | tf_op jit(solution)/shard_map/ppermute | solution.py:14
  288.2 10.6 %collective-permute-start.1 = (bf16[8,128,128]{2,1,0:T(8,128)(2,1)S(1)}, bf16[8,128,128]{2,1,0:T(8,128)(2,1)S(1)}, u32[]{:S(2)}, u32[]{:S(2)}) collective-permute-start(bf16[8,128,128]{2,1,0:T(8,128)(2,1)S(1)} %get-tuple-element.158), channel_id=1, source_target_pairs={{1,0},{2,1},{3,2},{4,3},{5,4},{6,5},{7,6},{8,7},{9,8},{10,9},{11,1... | collective-permute-start | bytes 786440 | tf_op jit(solution)/shard_map/ppermute | solution.py:14
  289.7 9.9 %collective-permute-start.2 = (bf16[8,128,128]{2,1,0:T(8,128)(2,1)S(1)}, bf16[8,128,128]{2,1,0:T(8,128)(2,1)S(1)}, u32[]{:S(2)}, u32[]{:S(2)}) collective-permute-start(bf16[8,128,128]{2,1,0:T(8,128)(2,1)S(1)} %get-tuple-element.157), channel_id=1, source_target_pairs={{0,32},{32,64},{64,96},{96,128},{128,160},{160,192},{192,224},{1,3... | collective-permute-start | bytes 786440 | tf_op jit(solution)/shard_map/ppermute | solution.py:14
  293.2 7.1 collective-permute-start.3
  384.8 3.6 copy-start.2
  388.3 541.1 %all-reduce.6.cloned.1.call-start = ((), (), s32[]{:S(2)}) async-start(), calls=%async_computation.2 | async-start | bytes 262144 | tf_op jit(solution)/shard_map/psum | solution.py:27
  539.7 31.5 %copy-start.3 = (f32[32,128,128]{2,1,0:T(8,128)S(1)}, f32[32,128,128]{2,1,0:T(8,128)}, u32[]{:S(2)}) copy-start(f32[32,128,128]{2,1,0:T(8,128)} %copy.20) | copy-start | bytes 6291460
  572.2 12.0 %copy-start.4 = (bf16[4096,128]{1,0:T(8,128)(2,1)}, bf16[4096,128]{1,0:T(8,128)(2,1)S(1)}, u32[]{:S(2)}) copy-start(bf16[4096,128]{1,0:T(8,128)(2,1)S(1)} %convolution_convert_fusion) | copy-start | bytes 3145732
  573.9 6.5 copy-start.7
  575.4 13.5 %collective-permute-start.4 = (bf16[8,128,128]{2,1,0:T(8,128)(2,1)S(1)}, bf16[8,128,128]{2,1,0:T(8,128)(2,1)S(1)}, u32[]{:S(2)}, u32[]{:S(2)}) collective-permute-start(bf16[8,128,128]{2,1,0:T(8,128)(2,1)S(1)} %get-tuple-element.155), channel_id=1, source_target_pairs={{0,1},{1,2},{2,3},{3,4},{4,5},{5,6},{6,7},{7,8},{8,9},{9,10},{10,1... | collective-permute-start | bytes 786440 | tf_op jit(solution)/shard_map/ppermute | solution.py:14
  578.8 10.8 %collective-permute-start.5 = (bf16[8,128,128]{2,1,0:T(8,128)(2,1)S(1)}, bf16[8,128,128]{2,1,0:T(8,128)(2,1)S(1)}, u32[]{:S(2)}, u32[]{:S(2)}) collective-permute-start(bf16[8,128,128]{2,1,0:T(8,128)(2,1)S(1)} %get-tuple-element.154), channel_id=1, source_target_pairs={{1,0},{2,1},{3,2},{4,3},{5,4},{6,5},{7,6},{8,7},{9,8},{10,9},{11,1... | collective-permute-start | bytes 786440 | tf_op jit(solution)/shard_map/ppermute | solution.py:14
  582.3 8.2 collective-permute-start.6
  585.3 7.5 collective-permute-start.7
  677.1 3.0 copy-start.5
  677.1 253.8 %copy-start.1 = (bf16[4096,128]{1,0:T(8,128)(2,1)S(1)}, bf16[4096,128]{1,0:T(8,128)(2,1)}, u32[]{:S(2)}) copy-start(bf16[4096,128]{1,0:T(8,128)(2,1)} %param.13) | copy-start | bytes 3145732
Sparse Core Ops, SparseCore 0:
  14.1 243.4 all-reduce.3
  388.4 137.1 all-gather.2
  682.3 247.0 all-reduce.5
